TPU v7x, 32 devices: a whole 2x2x4 slice. The times are simulated.
32 devices in a mesh: smp: 8 (over z, y), par: 4 (over x, core).
Axes of the slice: x: 2, y: 2, z: 4, core: 2. Of those that a mesh axis runs over, the one named last changes fastest.
Arguments:
- derivatives: bfloat16 [640, 2048], P('smp', 'par'), may hold values from -40 to 40
- epsilon: float32 [640], P('smp'), may hold values from -6 to 6
Outputs:
- gram_tile: float32 [640, 640], P('smp', 'par')
- update: float32 [2048], P('par')
All inputs are finite; a program needn't handle non-finite values.
Results may differ from a plain program's by a relative error of at most 0.003.
Values may be sent and summed in bfloat16 or wider, within the bound.
No kernel may reach another device: no remote copies, remote signals or barrier semaphores. Data moves between devices by JAX's collectives and lax.ppermute only.
A program may use at most 64 MiB of HBM per device.

v0:
```python
import math
import jax
import jax.numpy as jnp
from jax import lax
from jax.sharding import PartitionSpec as P


def shards(derivatives, epsilon):
    total_rows = derivatives.shape[0] * lax.axis_size("smp")
    factor = 1.0 / math.sqrt(total_rows)
    totals = lax.psum(jnp.sum(derivatives.astype(jnp.float32), axis=0), "smp")
    column_mean = totals / total_rows

    def center(values):
        return ((values.astype(jnp.float32) - column_mean) * factor).astype(jnp.bfloat16)

    own_rows = center(derivatives)
    partial_terms = jnp.dot(
        own_rows,
        center(lax.all_gather(derivatives, "smp", axis=0, tiled=True)).T,
        preferred_element_type=jnp.float32,
    )
    gram_tile = lax.psum_scatter(partial_terms, "par", scatter_dimension=1, tiled=True)
    local_sum = jnp.dot(epsilon, own_rows.astype(jnp.float32), precision=lax.Precision.HIGHEST)
    update = lax.psum(local_sum, "smp")
    return (gram_tile, update)


def solution(mesh):
    in_specs = (P("smp", "par"), P("smp"))
    out_specs = (P("smp", "par"), P("par"))
    return jax.shard_map(shards, mesh=mesh, in_specs=in_specs, out_specs=out_specs, check_vma=False)
```

profile of v0, /device:TPU:0, one launch (start us, length us, event | category | flops | bytes accessed | tf_op | source)
XLA Modules:
  0.0 90.6 jit_solution(17457802798909675866)
XLA Ops:
  7.2 0.0 copy-start
  7.2 0.0 copy-start.1
  7.2 0.0 reduce-scatter.4.cloned.1.call-start
  7.2 0.9 %convert_reduce_fusion = f32[512]{0:T(512)S(1)} fusion(bf16[80,512]{1,0:T(8,128)(2,1)} %param.2), kind=kLoop, calls=%fused_computation.5 | loop fusion | flops 81408 | bytes 83968 | tf_op jit(solution)/shard_map/reduce_sum | solution.py:11
  8.2 33.6 %all_gather.3 = bf16[640,512]{1,0:T(8,128)(2,1)S(1)} all-gather(bf16[80,512]{1,0:T(8,128)(2,1)} %param.2), channel_id=1, replica_groups=mesh['smp'=8,'par'=4] {'smp'}, dimensions={0}, use_global_device_ids=true | all-gather | bytes 737280 | tf_op jit(solution)/shard_map/all_gather | solution.py:20
  41.8 21.4 %psum.14 = f32[512]{0:T(512)S(1)} all-reduce(f32[512]{0:T(512)S(1)} %convert_reduce_fusion), channel_id=1, replica_groups=mesh['smp'=8,'par'=4] {'smp'}, use_global_device_ids=true, to_apply=%region_1.0 | all-reduce | flops 512 | bytes 4096 | tf_op jit(solution)/shard_map/psum | solution.py:11
  63.2 0.0 copy-done.1
  63.2 1.1 %convolution_bitcast_fusion = f32[640,80]{1,0:T(8,128)} fusion(bf16[640,512]{1,0:T(8,128)(2,1)S(1)} %all_gather.3, f32[512]{0:T(512)S(1)} %broadcast_multiply_fusion, bf16[80,512]{1,0:T(8,128)(2,1)S(1)} %copy-done.1), kind=kOutput, calls=%fused_computation.1 | convolution fusion | flops 53903360 | bytes 944128
  64.3 0.0 reduce-scatter.4.cloned.1.call-update
  64.3 0.0 copy-done
  64.3 0.2 fusion.4
  64.5 17.7 %psum.15 = f32[512]{0:T(512)} all-reduce(f32[512]{0:T(512)S(1)} %bitcast.8), channel_id=1, replica_groups=mesh['smp'=8,'par'=4] {'smp'}, use_global_device_ids=true, to_apply=%region_3.0 | all-reduce | flops 512 | bytes 4096 | tf_op jit(solution)/shard_map/psum | solution.py:25
  82.2 0.0 reduce-scatter.4.cloned.1.call-done
  82.2 1.6 %copy.5 = f32[80,160]{1,0:T(8,128)} copy(f32[80,160]{0,1:T(8,128)} %bitcast.7) | data formatting | bytes 102400
  (1 shorter events, 0.0 us)
Async XLA Ops:
  7.2 57.2 %copy-start = (f32[80]{0:T(128)S(1)}, f32[80]{0:T(128)}, u32[]{:S(2)}) copy-start(f32[80]{0:T(128)} %param.3) | copy-start | bytes 964
  7.2 56.1 %copy-start.1 = (bf16[80,512]{1,0:T(8,128)(2,1)S(1)}, bf16[80,512]{1,0:T(8,128)(2,1)}, u32[]{:S(2)}) copy-start(bf16[80,512]{1,0:T(8,128)(2,1)} %param.2) | copy-start | bytes 245764
  7.2 75.0 %reduce-scatter.4.cloned.1.call-start = ((), (), s32[]{:S(2)}) async-start(), calls=%async_computation.1 | async-start | bytes 409600
Sparse Core Ops, SparseCore 0:
  64.4 17.6 reduce-scatter.3
where the time goes:
time: 90.9 us; the launch traced here: 90.6 us
  blocking collectives  72.8 us (80%)
  between operations  14.1 us (16%)
  local copies, waits for them, and re-layouts  1.62 us (2%)
  matrix products  1.21 us (1%)
  other arithmetic  0.94 us (1%)
    all_gather x1, blocking collectives, shards(): lax.all_gather(derivatives, 'smp', axis=0, tiled=True)  33.6 us
    psum x1, blocking collectives, shards(): totals = lax.psum(jnp.sum(derivatives.astype(jnp.float32), axis=0), 'smp')  21.4 us
    psum x1, blocking collectives, shards(): update = lax.psum(local_sum, 'smp')  17.7 us
  transfers between devices with their start and end apart: 1, of which 0 were waited for; matrix products, arithmetic and copies ran while one was open for 0% of the time, Pallas kernels for 0%

commit v1 on v0

--- a/solution.py
+++ b/solution.py
@@ -6,6 +6,11 @@
 
 
 def shards(derivatives, epsilon):
+
+    def map_outputs(block_here):
+        carry_in = jnp.sum(jax.lax.all_gather(block_here, "smp"), axis=0)
+        return carry_in
+
     total_rows = derivatives.shape[0] * lax.axis_size("smp")
     factor = 1.0 / math.sqrt(total_rows)
     totals = lax.psum(jnp.sum(derivatives.astype(jnp.float32), axis=0), "smp")
@@ -22,7 +27,7 @@
     )
     gram_tile = lax.psum_scatter(partial_terms, "par", scatter_dimension=1, tiled=True)
     local_sum = jnp.dot(epsilon, own_rows.astype(jnp.float32), precision=lax.Precision.HIGHEST)
-    update = lax.psum(local_sum, "smp")
+    update = map_outputs(local_sum)
     return (gram_tile, update)
 
 

time: 90.9 us -> 99.9 us (1.099)
  blocking collectives: 72.8 us -> 81.2 us
    all_gather x0 -> x1, blocking collectives: none -> 26.1 us  [map_outputs(): carry_in = jnp.sum(jax.lax.all_gather(block_here, 'smp'), axis=0)]
    psum x1 -> x0, blocking collectives: 17.7 us -> none  [shards(): update = lax.psum(local_sum, 'smp')]
  transfers between devices with their start and end apart: 1 -> 1, of which waited for: 0 -> 0; matrix products, arithmetic and copies ran while one was open for 0% -> 1% of each run, Pallas kernels for 0% -> 0%
where the time goes in v1:
time: 99.9 us; the launch traced here: 99.7 us
  blocking collectives  81.2 us (81%)
  between operations  14.1 us (14%)
  local copies, waits for them, and re-layouts  1.62 us (2%)
  other arithmetic  1.55 us (2%)
  matrix products  1.21 us (1%)
    all_gather x1, blocking collectives, shards(): lax.all_gather(derivatives, 'smp', axis=0, tiled=True)  33.6 us
    all_gather x1, blocking collectives, map_outputs(): carry_in = jnp.sum(jax.lax.all_gather(block_here, 'smp'), axis=0)  26.1 us
    psum x1, blocking collectives, shards(): totals = lax.psum(jnp.sum(derivatives.astype(jnp.float32), axis=0), 'smp')  21.4 us
  transfers between devices with their start and end apart: 1, of which 0 were waited for; matrix products, arithmetic and copies ran while one was open for 1% of the time, Pallas kernels for 0%

profile of v1, /device:TPU:0, one launch (start us, length us, event | category | flops | bytes accessed | tf_op | source)
XLA Modules:
  0.0 99.7 jit_solution(472637263263299209)
XLA Ops:
  7.2 0.0 copy-start
  7.2 0.0 copy-start.1
  7.2 0.0 reduce-scatter.4.cloned.1.call-start
  7.2 0.9 convert_reduce_fusion
  8.2 33.6 %all_gather.9 = bf16[640,512]{1,0:T(8,128)(2,1)S(1)} all-gather(bf16[80,512]{1,0:T(8,128)(2,1)} %param.2), channel_id=1, replica_groups=mesh['smp'=8,'par'=4] {'smp'}, dimensions={0}, use_global_device_ids=true | all-gather | bytes 737280 | tf_op jit(solution)/shard_map/all_gather | solution.py:25
  41.8 21.4 %psum.7 = f32[512]{0:T(512)S(1)} all-reduce(f32[512]{0:T(512)S(1)} %convert_reduce_fusion), channel_id=1, replica_groups=mesh['smp'=8,'par'=4] {'smp'}, use_global_device_ids=true, to_apply=%region_1.0 | all-reduce | flops 512 | bytes 4096 | tf_op jit(solution)/shard_map/psum | solution.py:16
  63.2 0.0 copy-done.1
  63.2 1.1 %convolution_bitcast_fusion = f32[640,80]{1,0:T(8,128)} fusion(bf16[640,512]{1,0:T(8,128)(2,1)S(1)} %all_gather.9, f32[512]{0:T(512)S(1)} %broadcast_multiply_fusion, bf16[80,512]{1,0:T(8,128)(2,1)S(1)} %copy-done.1), kind=kOutput, calls=%fused_computation.1 | convolution fusion | flops 53903360 | bytes 944128
  64.3 0.0 reduce-scatter.4.cloned.1.call-update
  64.3 0.0 copy-done
  64.3 0.2 convolution_bitcast_fusion.1
  64.5 26.1 %all-gather.1 = f32[8,1,512]{2,1,0:T(1,128)S(1)} all-gather(f32[1,1,512]{2,1,0:T(1,128)S(1)} %convolution_bitcast_fusion.1), channel_id=2, replica_groups=mesh['smp'=8,'par'=4] {'smp'}, dimensions={0}, use_global_device_ids=true | all-gather | bytes 18432 | tf_op jit(solution)/shard_map/all_gather | solution.py:11
  90.6 0.6 reduce_sum.19
  91.2 0.0 reduce-scatter.4.cloned.1.call-done
  91.2 1.6 %copy.5 = f32[80,160]{1,0:T(8,128)} copy(f32[80,160]{0,1:T(8,128)} %bitcast.10) | data formatting | bytes 102400
  (1 shorter events, 0.0 us)
Async XLA Ops:
  7.2 57.2 %copy-start = (f32[80]{0:T(128)S(1)}, f32[80]{0:T(128)}, u32[]{:S(2)}) copy-start(f32[80]{0:T(128)} %param.3) | copy-start | bytes 964
  7.2 56.1 %copy-start.1 = (bf16[80,512]{1,0:T(8,128)(2,1)S(1)}, bf16[80,512]{1,0:T(8,128)(2,1)}, u32[]{:S(2)}) copy-start(bf16[80,512]{1,0:T(8,128)(2,1)} %param.2) | copy-start | bytes 245764
  7.2 84.0 %reduce-scatter.4.cloned.1.call-start = ((), (), s32[]{:S(2)}) async-start(), calls=%async_computation.1 | async-start | bytes 409600
Sparse Core Ops, SparseCore 0:
  64.4 17.6 reduce-scatter.3
